TPU v7x, 32 devices: a whole 2x2x4 slice. The times are simulated.
32 devices in a mesh: gx: 16 (over z, y, x), gy: 2 (over core).
Axes of the slice: x: 2, y: 2, z: 4, core: 2. Of those that a mesh axis runs over, the one named last changes fastest.
Arguments:
- features: bfloat16 [16, 2, 8, 128, 256], P('gx', 'gy'), may hold values from -6 to 6
- kernel_weight: bfloat16 [27, 256, 256], P(None, 'gy'), may hold values from -0.109375 to 0.109375
- channel_bias: float32 [256], replicated, may hold values from -3 to 3
- send_list: int32 [16, 2, 2], P('gx', 'gy'), may hold values from 0 to 7
- rule_source: int32 [16, 2, 27, 4], P('gx', 'gy'), may hold values from 0 to 23
- rule_target: int32 [16, 2, 27, 4], P('gx', 'gy'), may hold values from 0 to 7
- live_counts: int32 [16, 2, 27], P('gx', 'gy'), may hold values from 1 to 4, as said below
- out_grad: bfloat16 [16, 2, 8, 128, 256], P('gx', 'gy'), may hold values from -6 to 6
Outputs:
- outputs: bfloat16 [16, 2, 8, 128, 256], P('gx', 'gy')
- feat_grad: bfloat16 [16, 2, 8, 128, 256], P('gx', 'gy')
- weight_grad: float32 [27, 256, 256], P(None, 'gy')
Inputs may be any that keep to these rules, and one draw needn't show every extreme that they name: `rule_source`: index into the device's block table of its 8 own blocks followed by 2 blocks from each of the eight directions. `rule_target`: an own block of the device. `send_list`: an own block of the device; a block may appear more than once. `live_counts`: slots from this count up to 3 are padding whose indices carry no meaning.
All inputs are finite; a program needn't handle non-finite values.
Results may differ from a plain program's by a relative error of at most 0.007.
Values may be sent and summed in bfloat16 or wider, within the bound.
A program may use at most 128 MiB of HBM per device.

v0:
```python
import functools

import jax
import jax.numpy as jnp
from jax import lax
from jax.experimental import pallas as pl
from jax.experimental.pallas import tpu as pltpu
from jax.sharding import PartitionSpec as P

MESH = pl.DeviceIdType.MESH
VMEM = pltpu.VMEM
SMEM = pltpu.SMEM
DIRECTIONS = [(sx, sy) for sx in (-1, 0, 1) for sy in (-1, 0, 1) if (sx, sy) != (0, 0)]
LANES = 128
TILE = 16
GROUPS = 9
ROTATIONS = 3


def inside(i, j, nx, ny):
    return (i >= 0) & (i < nx) & (j >= 0) & (j < ny)


def clipped(i, j, nx, ny):
    return jnp.clip(i, 0, nx - 1), jnp.clip(j, 0, ny - 1)


def greet_neighbours(barrier, me_x, me_y, nx, ny):
    total = 0
    for sx, sy in DIRECTIONS:
        there = inside(me_x + sx, me_y + sy, nx, ny)

        @pl.when(there)
        def _():
            pl.semaphore_signal(
                barrier, inc=1, device_id=(me_x + sx, me_y + sy), device_id_type=MESH
            )

        total = total + there.astype(jnp.int32)
    return total


def greet_column(barrier, me_x, me_y, ny):
    for step in range(1, ny):
        pl.semaphore_signal(
            barrier, inc=1, device_id=(me_x, lax.rem(me_y + step, ny)), device_id_type=MESH
        )
    return ny - 1


def exchange_kernel(
    nx, ny, send_ref, feats_ref, weight_ref, halo_ref, full_ref, shared, hsend, hrecv, wsend, wrecv
):
    me_x, me_y = lax.axis_index("gx"), lax.axis_index("gy")
    barrier = pltpu.get_barrier_semaphore()
    expected = greet_neighbours(barrier, me_x, me_y, nx, ny) + greet_column(
        barrier, me_x, me_y, ny
    )
    for s in range(shared.shape[0]):
        shared[s] = feats_ref[send_ref[s]]
    pl.semaphore_wait(barrier, expected)

    def halo_copy(d, i, j):
        return pltpu.make_async_remote_copy(
            src_ref=shared,
            dst_ref=halo_ref.at[d],
            send_sem=hsend.at[d],
            recv_sem=hrecv.at[d],
            device_id=(i, j),
            device_id_type=MESH,
        )

    def weight_copy(step, owner):
        return pltpu.make_async_remote_copy(
            src_ref=weight_ref,
            dst_ref=full_ref.at[:, owner],
            send_sem=wsend.at[step],
            recv_sem=wrecv.at[step],
            device_id=(me_x, lax.rem(me_y + step, ny)),
            device_id_type=MESH,
        )

    for d, (sx, sy) in enumerate(DIRECTIONS):

        @pl.when(inside(me_x - sx, me_y - sy, nx, ny))
        def _():
            halo_copy(d, me_x - sx, me_y - sy).start()

    for step in range(1, ny):
        weight_copy(step, me_y).start()
    full_ref[:, me_y] = weight_ref[...]
    for d, (sx, sy) in enumerate(DIRECTIONS):
        there = inside(me_x + sx, me_y + sy, nx, ny)

        @pl.when(jnp.logical_not(there))
        def _():
            halo_ref[d] = jnp.zeros(halo_ref.shape[1:], halo_ref.dtype)

        @pl.when(there)
        def _():
            halo_copy(d, me_x + sx, me_y + sy).wait_recv()

        @pl.when(inside(me_x - sx, me_y - sy, nx, ny))
        def _():
            halo_copy(d, me_x - sx, me_y - sy).wait_send()

    for step in range(1, ny):
        weight_copy(step, lax.rem(me_y - step + ny, ny)).wait_recv()
        weight_copy(step, me_y).wait_send()


def compute_kernel(
    slots,
    source_ref,
    target_ref,
    count_ref,
    feats_ref,
    halo_ref,
    weight_ref,
    bias_ref,
    cot_ref,
    out_ref,
    own_ref,
    borrowed_ref,
    wpart_ref,
    table,
    pre,
    dpre,
    grad,
):
    blocks, rows, width = feats_ref.shape
    kvol = weight_ref.shape[0]
    ny, tiles = wpart_ref.shape[:2]
    share = width // ny
    share_tiles = share // TILE
    for b in range(blocks):
        table[b] = feats_ref[b]
        pre[b] = jnp.broadcast_to(bias_ref[...], (rows, width))
    for t in range(halo_ref.shape[0]):
        table[blocks + t] = halo_ref[t]
    for t in range(grad.shape[0]):
        grad[t] = jnp.zeros((rows, width), jnp.float32)

    def by_count(k, work):
        live = count_ref[k]
        for amount in range(1, slots + 1):

            @pl.when(live == amount)
            def _():
                work(
                    [source_ref[k * slots + q] for q in range(amount)],
                    [target_ref[k * slots + q] for q in range(amount)],
                )

    def forward(k, carry):
        def work(sources, targets):
            taken = jnp.concatenate([table[s] for s in sources], axis=0)
            made = jnp.dot(taken, weight_ref[k], preferred_element_type=jnp.float32)
            for q, target in enumerate(targets):
                pre[target] += made[q * rows : (q + 1) * rows]

        by_count(k, work)
        return carry

    lax.fori_loop(0, kvol, forward, 0)

    def activate(b, carry):
        value = pre[b]
        sig = jax.nn.sigmoid(value)
        out_ref[b] = (value * sig).astype(out_ref.dtype)
        dpre[b] = (cot_ref[b].astype(jnp.float32) * sig * (1.0 + value * (1.0 - sig))).astype(
            dpre.dtype
        )
        return carry

    lax.fori_loop(0, blocks, activate, 0)

    filled = 2 * kvol * share_tiles
    if filled < tiles:
        for y in range(ny):
            wpart_ref[y, filled:] = jnp.zeros((tiles - filled, TILE, LANES), wpart_ref.dtype)

    def backward(k, carry):
        def work(sources, targets):
            taken = jnp.concatenate([table[s] for s in sources], axis=0)
            pulled = jnp.concatenate([dpre[t] for t in targets], axis=0)
            back = lax.dot_general(
                pulled, weight_ref[k], (((1,), (1,)), ((), ())), preferred_element_type=jnp.float32
            )
            for q, source in enumerate(sources):
                grad[source] += back[q * rows : (q + 1) * rows]
            part = lax.dot_general(
                taken, pulled, (((0,), (0,)), ((), ())), preferred_element_type=jnp.float32
            ).astype(wpart_ref.dtype)
            for y in range(ny):
                for h in range(width // LANES):
                    piece = part[y * share : (y + 1) * share, h * LANES : (h + 1) * LANES]
                    wpart_ref[y, pl.ds((h * kvol + k) * share_tiles, share_tiles)] = piece.reshape(
                        share_tiles, TILE, LANES
                    )

        by_count(k, work)
        return carry

    lax.fori_loop(0, kvol, backward, 0)
    for b in range(blocks):
        own_ref[b] = grad[b]
    for t in range(borrowed_ref.shape[0]):
        borrowed_ref[t] = grad[blocks + t].astype(borrowed_ref.dtype)


def reduce_kernel(
    nx,
    ny,
    wpart_ref,
    borrowed_ref,
    sum_ref,
    returned_ref,
    work,
    yland,
    xland,
    hland,
    ysend,
    yrecv,
    rsend,
    rrecv,
    gsend,
    grecv,
    hsend,
    hrecv,
):
    me_x, me_y = lax.axis_index("gx"), lax.axis_index("gy")
    groups = work.shape[0]
    steps = nx.bit_length() - 1
    bits = [lax.rem(me_x // (1 << b), 2) for b in range(steps)]
    partners = [me_x + (1 - 2 * bits[b]) * (1 << b) for b in range(steps)]

    barrier = pltpu.get_barrier_semaphore()
    expected = greet_neighbours(barrier, me_x, me_y, nx, ny) + greet_column(
        barrier, me_x, me_y, ny
    )
    for b in range(steps):
        pl.semaphore_signal(barrier, inc=1, device_id=(partners[b], me_y), device_id_type=MESH)
    pl.semaphore_wait(barrier, expected + steps)

    def halo_copy(d, i, j):
        return pltpu.make_async_remote_copy(
            src_ref=borrowed_ref.at[d],
            dst_ref=hland.at[d],
            send_sem=hsend.at[d],
            recv_sem=hrecv.at[d],
            device_id=(i, j),
            device_id_type=MESH,
        )

    def column_copy(step, g):
        other = lax.rem(me_y + step, ny)
        return pltpu.make_async_remote_copy(
            src_ref=wpart_ref.at[other, g],
            dst_ref=yland.at[step - 1, g],
            send_sem=ysend.at[step - 1, g],
            recv_sem=yrecv.at[step - 1, g],
            device_id=(me_x, other),
            device_id_type=MESH,
        )

    orders = [[(s + g % ROTATIONS) % steps for s in range(steps)] for g in range(groups)]
    starts = []
    for g in range(groups):
        at = [0]
        for s in range(steps):
            at.append(at[-1] + bits[orders[g][s]] * (nx >> (s + 1)))
        starts.append(at)

    def scatter_copy(g, s):
        half = nx >> (s + 1)
        bit = bits[orders[g][s]]
        away = starts[g][s] + (1 - bit) * half
        return pltpu.make_async_remote_copy(
            src_ref=work.at[g, pl.ds(away, half)],
            dst_ref=xland.at[g, pl.ds(nx - 2 * half, half)],
            send_sem=rsend.at[s, g],
            recv_sem=rrecv.at[s, g],
            device_id=(partners[orders[g][s]], me_y),
            device_id_type=MESH,
        )

    def gather_copy(g, s, landing):
        half = nx >> (s + 1)
        bit = bits[orders[g][s]]
        mine = starts[g][s + 1]
        place = starts[g][s] + (1 - bit) * half if landing else mine
        return pltpu.make_async_remote_copy(
            src_ref=sum_ref.at[g, pl.ds(mine, half)],
            dst_ref=sum_ref.at[g, pl.ds(place, half)],
            send_sem=gsend.at[s, g],
            recv_sem=grecv.at[s, g],
            device_id=(partners[orders[g][s]], me_y),
            device_id_type=MESH,
        )

    for g in range(groups):
        for step in range(1, ny):
            column_copy(step, g).start()
    for d, (sx, sy) in enumerate(DIRECTIONS):

        @pl.when(inside(me_x + sx, me_y + sy, nx, ny))
        def _():
            halo_copy(d, me_x + sx, me_y + sy).start()

    for g in range(groups):
        value = wpart_ref[me_y, g].astype(jnp.float32)
        for step in range(1, ny):
            column_copy(step, g).wait_recv()
            value = value + yland[step - 1, g].astype(jnp.float32)
        work[g] = value.astype(work.dtype)
        scatter_copy(g, 0).start()

    for s in range(steps):
        half = nx >> (s + 1)
        for g in range(groups):
            scatter_copy(g, s).wait_recv()
            keep = pl.ds(starts[g][s + 1], half)
            value = work[g, keep].astype(jnp.float32) + xland[
                g, pl.ds(nx - 2 * half, half)
            ].astype(jnp.float32)
            if s < steps - 1:
                work[g, keep] = value.astype(work.dtype)
                scatter_copy(g, s + 1).start()
            else:
                sum_ref[g, keep] = value.astype(sum_ref.dtype)
                gather_copy(g, s, False).start()

    returned_ref[...] = jnp.zeros(returned_ref.shape, jnp.float32)
    for d, (sx, sy) in enumerate(DIRECTIONS):

        @pl.when(inside(me_x - sx, me_y - sy, nx, ny))
        def _():
            halo_copy(d, me_x - sx, me_y - sy).wait_recv()
            returned_ref[...] += hland[d].astype(jnp.float32)

    for s in reversed(range(steps)):
        for g in range(groups):
            gather_copy(g, s, True).wait_recv()
            if s > 0:
                gather_copy(g, s - 1, False).start()

    for g in range(groups):
        for step in range(1, ny):
            column_copy(step, g).wait_send()
        for s in range(steps):
            scatter_copy(g, s).wait_send()
            gather_copy(g, s, False).wait_send()
    for d, (sx, sy) in enumerate(DIRECTIONS):

        @pl.when(inside(me_x + sx, me_y + sy, nx, ny))
        def _():
            halo_copy(d, me_x + sx, me_y + sy).wait_send()


def on_device(
    nx,
    ny,
    features,
    kernel_weight,
    channel_bias,
    send_list,
    rule_source,
    rule_target,
    live_counts,
    out_grad,
):
    feats = features[0, 0]
    blocks, rows, width = feats.shape
    shared = send_list[0, 0]
    shared_count = shared.shape[0]
    kvol, slots = rule_source.shape[2:]
    share = kernel_weight.shape[1]
    bf16, f32 = jnp.bfloat16, jnp.float32
    shape = jax.ShapeDtypeStruct
    vmem = pl.BlockSpec(memory_space=VMEM)
    smem = pl.BlockSpec(memory_space=SMEM)
    directions = len(DIRECTIONS)
    dma = pltpu.SemaphoreType.DMA

    halo, full = pl.pallas_call(
        functools.partial(exchange_kernel, nx, ny),
        out_shape=(
            shape((directions, shared_count, rows, width), bf16),
            shape((kvol, ny, share, width), bf16),
        ),
        in_specs=[smem, vmem, vmem],
        out_specs=(vmem, vmem),
        scratch_shapes=[
            VMEM((shared_count, rows, width), bf16),
            dma((directions,)),
            dma((directions,)),
            dma((ny,)),
            dma((ny,)),
        ],
        compiler_params=pltpu.CompilerParams(collective_id=0, has_side_effects=True),
    )(shared, feats, kernel_weight)

    borrowed_count = directions * shared_count
    used = (width // LANES) * kvol * (share // TILE)
    unit = GROUPS * nx
    tiles = -(-used // unit) * unit
    depth = tiles // unit
    outputs, own, borrowed, wpart = pl.pallas_call(
        functools.partial(compute_kernel, slots),
        out_shape=(
            shape((blocks, rows, width), bf16),
            shape((blocks, rows, width), f32),
            shape((borrowed_count, rows, width), bf16),
            shape((ny, tiles, TILE, LANES), bf16),
        ),
        in_specs=[smem, smem, smem, vmem, vmem, vmem, vmem, vmem],
        out_specs=(vmem, vmem, vmem, vmem),
        scratch_shapes=[
            VMEM((blocks + borrowed_count, rows, width), bf16),
            VMEM((blocks, rows, width), f32),
            VMEM((blocks, rows, width), bf16),
            VMEM((blocks + borrowed_count, rows, width), f32),
        ],
    )(
        rule_source.reshape(-1),
        rule_target.reshape(-1),
        live_counts.reshape(-1),
        feats,
        halo.reshape(borrowed_count, rows, width),
        full.reshape(kvol, width, width),
        channel_bias.reshape(1, width),
        out_grad[0, 0],
    )

    steps = nx.bit_length() - 1
    block = (depth, TILE, LANES)
    total, returned = pl.pallas_call(
        functools.partial(reduce_kernel, nx, ny),
        out_shape=(
            shape((GROUPS, nx) + block, bf16),
            shape((shared_count, rows, width), f32),
        ),
        in_specs=[vmem, vmem],
        out_specs=(vmem, vmem),
        scratch_shapes=[
            VMEM((GROUPS, nx) + block, bf16),
            VMEM((max(ny - 1, 1), GROUPS, nx) + block, bf16),
            VMEM((GROUPS, nx) + block, bf16),
            VMEM((directions, shared_count, rows, width), bf16),
            dma((max(ny - 1, 1), GROUPS)),
            dma((max(ny - 1, 1), GROUPS)),
            dma((steps, GROUPS)),
            dma((steps, GROUPS)),
            dma((steps, GROUPS)),
            dma((steps, GROUPS)),
            dma((directions,)),
            dma((directions,)),
        ],
        compiler_params=pltpu.CompilerParams(collective_id=1, has_side_effects=True),
    )(
        wpart.reshape((ny, GROUPS, nx) + block),
        borrowed.reshape(directions, shared_count, rows, width),
    )

    weight_grad = (
        total.reshape(tiles, TILE, LANES)[:used]
        .reshape(width // LANES, kvol, share, LANES)
        .transpose(1, 2, 0, 3)
        .reshape(kvol, share, width)
        .astype(f32)
    ) * (1.0 / rows)
    feat_grad = own
    for s in range(shared_count):
        hit = shared[s] == jnp.arange(blocks, dtype=jnp.int32)
        feat_grad = feat_grad + jnp.where(hit[:, None, None], returned[s][None], 0.0)
    return (outputs[None, None], feat_grad.astype(bf16)[None, None], weight_grad)


def solution(mesh):
    return jax.shard_map(
        functools.partial(on_device, mesh.shape["gx"], mesh.shape["gy"]),
        mesh=mesh,
        in_specs=(
            P("gx", "gy", None, None, None),
            P(None, "gy", None),
            P(),
            P("gx", "gy", None),
            P("gx", "gy", None, None),
            P("gx", "gy", None, None),
            P("gx", "gy", None),
            P("gx", "gy", None, None, None),
        ),
        out_specs=(
            P("gx", "gy", None, None, None),
            P("gx", "gy", None, None, None),
            P(None, "gy", None),
        ),
        check_vma=False,
    )
```

profile of v0, /device:TPU:0, one launch (start us, length us, event | category | flops | bytes accessed | tf_op | source)
XLA Modules:
  0.0 109.7 jit_solution(6342824129720161594)
XLA Ops:
  0.6 20.6 %shard_map.103 = (bf16[8,2,128,256]{3,2,1,0:T(8,128)(2,1)}, bf16[27,2,128,256]{3,2,1,0:T(8,128)(2,1)}) custom-call(s32[2]{0:T(128)} %bitcast.34, bf16[8,128,256]{2,1,0:T(8,128)(2,1)} %bitcast.29, bf16[27,128,256]{2,1,0:T(8,128)(2,1)} %weight_ref.1), custom_call_target="tpu_custom_call" | custom-call | tf_op jit(solution)/shard_map/pallas_call | solution.py:386
  21.2 0.8 copy.14
  22.0 0.6 reshape.49.source_ref
  22.6 0.8 copy.15
  23.4 0.6 reshape.50.target_ref
  24.0 19.2 %shard_map.104 = (bf16[8,128,256]{2,1,0:T(8,128)(2,1)}, f32[8,128,256]{2,1,0:T(8,128)}, bf16[16,128,256]{2,1,0:T(8,128)(2,1)}, bf16[2,432,16,128]{3,2,1,0:T(8,128)(2,1)}) custom-call(s32[108]{0:T(128)} %reshape.49.source_ref, s32[108]{0:T(128)} %reshape.50.target_ref, s32[27]{0:T(128)} %bitcast.36, bf16[8,128,256]{2,1,0:T(8,128)(2,1)} %bitcast.30, ...), custom_call_target="tpu_custom_call" | custom-call | tf_op jit(solution)/shard_map/pallas_call | solution.py:409
  43.2 0.0 copy-start.2
  43.2 0.0 copy-start.1
  43.2 59.9 %shard_map.105 = (bf16[9,16,3,16,128]{4,3,2,1,0:T(8,128)(2,1)}, f32[2,128,256]{2,1,0:T(8,128)}) custom-call(bf16[2,9,16,3,16,128]{5,4,3,2,1,0:T(8,128)(2,1)} %bitcast.27, bf16[8,2,128,256]{3,2,1,0:T(8,128)(2,1)} %bitcast.32), custom_call_target="tpu_custom_call" | custom-call | tf_op jit(solution)/shard_map/pallas_call | solution.py:438
  103.1 0.0 copy-start
  103.1 1.1 %slice_bitcast_fusion.1 = (f32[128,256]{1,0:T(8,128)S(1)}, f32[128,256]{1,0:T(8,128)S(1)}) fusion(f32[2,128,256]{2,1,0:T(8,128)} %get-tuple-element.17), kind=kLoop, calls=%fused_computation.5 | loop fusion | bytes 524288 | tf_op jit(solution)/shard_map/jit(_where)/broadcast_in_dim | solution.py:476
  104.3 0.0 copy-done.2
  104.3 0.6 fusion.1
  104.9 1.3 %iota_compare_fusion = (pred[8]{0:T(512)(128)(4,1)S(1)}, pred[8]{0:T(512)(128)(4,1)S(1)}) fusion(s32[]{:T(128)} %bitcast.12, s32[]{:T(128)} %bitcast.8), kind=kLoop, calls=%fused_computation.6 | loop fusion | flops 16 | bytes 24 | tf_op jit(solution)/shard_map/eq | solution.py:475
  106.2 0.0 copy-done.1
  106.2 1.0 fusion
  107.2 0.0 copy-done
  107.2 0.3 convert_multiply_fusion
  107.5 2.1 %copy.19 = f32[2,27,16,8,128]{4,3,0,2,1:T(8,128)} copy(f32[2,27,16,8,128]{4,3,2,1,0:T(8,128)S(1)} %bitcast.25) | data formatting | bytes 7077888 | tf_op jit(solution)/shard_map/mul | solution.py:466
Async XLA Ops:
  43.2 61.0 %copy-start.2 = (s32[1,1,2]{2,1,0:T(1,128)S(1)}, s32[1,1,2]{2,1,0:T(1,128)}, u32[]{:S(2)}) copy-start(s32[1,1,2]{2,1,0:T(1,128)} %param.11) | copy-start | bytes 28
  43.2 62.9 %copy-start.1 = (f32[8,128,256]{2,1,0:T(8,128)S(1)}, f32[8,128,256]{2,1,0:T(8,128)}, u32[]{:S(2)}) copy-start(f32[8,128,256]{2,1,0:T(8,128)} %get-tuple-element.14) | copy-start | bytes 3145732
  103.1 4.1 %copy-start = (bf16[9,16,3,16,128]{4,3,2,1,0:T(8,128)(2,1)S(1)}, bf16[9,16,3,16,128]{4,3,2,1,0:T(8,128)(2,1)}, u32[]{:S(2)}) copy-start(bf16[9,16,3,16,128]{4,3,2,1,0:T(8,128)(2,1)} %get-tuple-element.18) | copy-start | bytes 5308420
where the time goes:
time: 109 us; the launch traced here: 110 us
  Pallas kernels  99.7 us (91%)
  local copies, waits for them, and re-layouts  6.6 us (6%)
  other arithmetic  2.66 us (2%)
    pallas_call x1, Pallas kernels, on_device(): pl.pallas_call(functools.partial(reduce_kernel, nx, ny), out_shape=(shape...  59.9 us
    pallas_call x1, Pallas kernels, on_device(): pl.pallas_call(functools.partial(exchange_kernel, nx, ny), out_shape=(sha...  20.6 us
    pallas_call x1, Pallas kernels, on_device(): pl.pallas_call(functools.partial(compute_kernel, slots), out_shape=(shape...  19.2 us

commit v1 on v0

v1 whole, which is shorter than its diff:
```python
import functools

import jax
import jax.numpy as jnp
from jax import lax
from jax.experimental import pallas as pl
from jax.experimental.pallas import tpu as pltpu
from jax.sharding import PartitionSpec as P

MESH = pl.DeviceIdType.MESH
VMEM = pltpu.VMEM
SMEM = pltpu.SMEM
LANES = 128
TILE = 16
KINDS = (2, 0, 1, 3, 0, 1, 0, 1, 0)
UNROLL = 3
VMEM_BYTES = 28 * 1024 * 1024


def greet_neighbours(barrier, me_x, me_y, nx, ny):
    total = 0
    for sx, sy in ((-1, 0), (1, 0), (0, -1), (0, 1)):
        x, y = me_x + sx, me_y + sy
        there = (x >= 0) & (x < nx) & (y >= 0) & (y < ny)

        @pl.when(there)
        def _():
            pl.semaphore_signal(barrier, inc=1, device_id=(x, y), device_id_type=MESH)

        total = total + there.astype(jnp.int32)
    return total


def greet_column(barrier, me_x, me_y, ny):
    for step in range(1, ny):
        pl.semaphore_signal(
            barrier, inc=1, device_id=(me_x, lax.rem(me_y + step, ny)), device_id_type=MESH
        )
    return ny - 1


def exists(index, count):
    return (index >= 0) & (index < count)


def exchange_kernel(
    nx, ny, send_ref, feats_ref, weight_ref, halo_ref, full_ref, xsend, xrecv, hsend, hrecv, wsend, wrecv
):
    me_x, me_y = lax.axis_index("gx"), lax.axis_index("gy")
    barrier = pltpu.get_barrier_semaphore()
    expected = greet_neighbours(barrier, me_x, me_y, nx, ny) + greet_column(
        barrier, me_x, me_y, ny
    )
    for s in range(halo_ref.shape[1]):
        halo_ref[4, s] = feats_ref[send_ref[s]]
    pl.semaphore_wait(barrier, expected)

    def x_copy(a, device_x):
        return pltpu.make_async_remote_copy(
            src_ref=halo_ref.at[4],
            dst_ref=halo_ref.at[3 * a + 1],
            send_sem=xsend.at[a // 2],
            recv_sem=xrecv.at[a // 2],
            device_id=(device_x, me_y),
            device_id_type=MESH,
        )

    def y_copy(a, b, device_y):
        return pltpu.make_async_remote_copy(
            src_ref=halo_ref.at[3 * a + 1],
            dst_ref=halo_ref.at[3 * a + b],
            send_sem=hsend.at[a, b // 2],
            recv_sem=hrecv.at[a, b // 2],
            device_id=(me_x, device_y),
            device_id_type=MESH,
        )

    def weight_copy(step, owner):
        return pltpu.make_async_remote_copy(
            src_ref=weight_ref,
            dst_ref=full_ref.at[:, owner],
            send_sem=wsend.at[step],
            recv_sem=wrecv.at[step],
            device_id=(me_x, lax.rem(me_y + step, ny)),
            device_id_type=MESH,
        )

    def to_column(a, act):
        for b in (0, 2):
            target = me_y + 1 - b

            @pl.when(exists(target, ny))
            def _():
                act(y_copy(a, b, target))

    for a in (0, 2):
        target = me_x + 1 - a

        @pl.when(exists(target, nx))
        def _():
            x_copy(a, target).start()

    to_column(1, lambda copy: copy.start())
    for step in range(1, ny):
        weight_copy(step, me_y).start()
    full_ref[:, me_y] = weight_ref[...]
    blank = jnp.zeros(halo_ref.shape[1:], halo_ref.dtype)
    for a in (0, 2):
        here = exists(me_x + a - 1, nx)

        @pl.when(jnp.logical_not(here))
        def _():
            halo_ref[3 * a + 1] = blank

        @pl.when(here)
        def _():
            x_copy(a, me_x + a - 1).wait_recv()
            to_column(a, lambda copy: copy.start())

    for a in range(3):
        for b in (0, 2):
            there = exists(me_x + a - 1, nx) & exists(me_y + b - 1, ny)

            @pl.when(jnp.logical_not(there))
            def _():
                halo_ref[3 * a + b] = blank

            @pl.when(there)
            def _():
                y_copy(a, b, me_y + b - 1).wait_recv()

        @pl.when(exists(me_x + a - 1, nx))
        def _():
            to_column(a, lambda copy: copy.wait_send())

    for a in (0, 2):
        target = me_x + 1 - a

        @pl.when(exists(target, nx))
        def _():
            x_copy(a, target).wait_send()

    for step in range(1, ny):
        weight_copy(step, lax.rem(me_y - step + ny, ny)).wait_recv()
        weight_copy(step, me_y).wait_send()


def compute_kernel(
    source_ref,
    target_ref,
    count_ref,
    feats_ref,
    halo_ref,
    weight_ref,
    bias_ref,
    cot_ref,
    out_ref,
    own_ref,
    borrowed_ref,
    wpart_ref,
    table,
    turned,
    pre,
    dpre,
    grad,
):
    blocks, rows, width = feats_ref.shape
    slots = source_ref.shape[0]
    kvol = weight_ref.shape[0]
    total_blocks = grad.shape[0] - 1
    shared_count = halo_ref.shape[1]
    ny, tiles = wpart_ref.shape[:2]
    share = width // ny
    share_tiles = share // TILE
    places = [(b, feats_ref.at[b]) for b in range(blocks)]
    at = blocks
    for d in range(9):
        if d != 4:
            for s in range(shared_count):
                places.append((at, halo_ref.at[d, s]))
                at += 1
    for t, ref in places:
        value = ref[...]
        table[t] = value
        turned[t] = value.T
    for b in range(blocks):
        pre[b] = jnp.broadcast_to(bias_ref[...], (rows, width))
    for t in range(total_blocks):
        grad[t] = jnp.zeros((rows, width), jnp.float32)
    pre[blocks] = jnp.zeros((rows, width), jnp.float32)
    grad[total_blocks] = jnp.zeros((rows, width), jnp.float32)
    dpre[blocks] = jnp.zeros((rows, width), dpre.dtype)

    def rules(k):
        live = count_ref[k]
        sources = [source_ref[q, k] for q in range(slots)]
        targets = [target_ref[q, k] for q in range(slots)]
        reads = [jnp.where(q < live, v, 0) for q, v in enumerate(sources)]
        spread = [jnp.where(q < live, v, total_blocks) for q, v in enumerate(sources)]
        targets = [jnp.where(q < live, v, blocks) for q, v in enumerate(targets)]
        return reads, spread, targets

    def forward(k, carry):
        reads, _, targets = rules(k)
        taken = jnp.concatenate([table[s] for s in reads], axis=0)
        made = jnp.dot(taken, weight_ref[k], preferred_element_type=jnp.float32)
        for q, target in enumerate(targets):
            pre[target] += made[q * rows : (q + 1) * rows]
        return carry

    lax.fori_loop(0, kvol, forward, 0, unroll=UNROLL)

    def activate(b, carry):
        value = pre[b]
        sig = jax.nn.sigmoid(value)
        out_ref[b] = (value * sig).astype(out_ref.dtype)
        dpre[b] = (cot_ref[b].astype(jnp.float32) * sig * (1.0 + value * (1.0 - sig))).astype(
            dpre.dtype
        )
        return carry

    lax.fori_loop(0, blocks, activate, 0)

    filled = 2 * kvol * share_tiles
    if filled < tiles:
        for y in range(ny):
            wpart_ref[y, filled:] = jnp.zeros((tiles - filled, TILE, LANES), wpart_ref.dtype)

    def backward(k, carry):
        reads, spread, targets = rules(k)
        pulled = jnp.concatenate([dpre[t] for t in targets], axis=0)
        taken = jnp.concatenate([turned[s] for s in reads], axis=1)
        part = jnp.dot(taken, pulled, preferred_element_type=jnp.float32).astype(wpart_ref.dtype)
        for y in range(ny):
            for h in range(width // LANES):
                piece = part[y * share : (y + 1) * share, h * LANES : (h + 1) * LANES]
                wpart_ref[y, pl.ds((h * kvol + k) * share_tiles, share_tiles)] = piece.reshape(
                    share_tiles, TILE, LANES
                )
        back = lax.dot_general(
            pulled, weight_ref[k], (((1,), (1,)), ((), ())), preferred_element_type=jnp.float32
        )
        for q, source in enumerate(spread):
            grad[source] += back[q * rows : (q + 1) * rows]
        return carry

    lax.fori_loop(0, kvol, backward, 0, unroll=UNROLL)
    for b in range(blocks):
        own_ref[b] = grad[b]
    at = blocks
    for d in range(9):
        for s in range(shared_count):
            if d == 4:
                borrowed_ref[d, s] = jnp.zeros((rows, width), borrowed_ref.dtype)
            else:
                borrowed_ref[d, s] = grad[at].astype(borrowed_ref.dtype)
                at += 1


def reduce_kernel(
    nx,
    ny,
    wpart_ref,
    borrowed_ref,
    sum_ref,
    returned_ref,
    work,
    yland,
    xland,
    side_land,
    column,
    x_land,
    ysend,
    yrecv,
    rsend,
    rrecv,
    gsend,
    grecv,
    hsend,
    hrecv,
    bsend,
    brecv,
):
    me_x, me_y = lax.axis_index("gx"), lax.axis_index("gy")
    groups = work.shape[0]
    steps = nx.bit_length() - 1
    bits = [lax.rem(me_x // (1 << b), 2) for b in range(steps)]
    partners = [me_x + (1 - 2 * bits[b]) * (1 << b) for b in range(steps)]

    barrier = pltpu.get_barrier_semaphore()
    expected = greet_neighbours(barrier, me_x, me_y, nx, ny) + greet_column(
        barrier, me_x, me_y, ny
    )
    for b in range(steps):
        pl.semaphore_signal(barrier, inc=1, device_id=(partners[b], me_y), device_id_type=MESH)
    pl.semaphore_wait(barrier, expected + steps)

    def side_copy(a, b):
        return pltpu.make_async_remote_copy(
            src_ref=borrowed_ref.at[3 * a + b],
            dst_ref=side_land.at[a, b // 2],
            send_sem=hsend.at[a, b // 2],
            recv_sem=hrecv.at[a, b // 2],
            device_id=(me_x, me_y + b - 1),
            device_id_type=MESH,
        )

    def back_copy(a):
        return pltpu.make_async_remote_copy(
            src_ref=column.at[a // 2],
            dst_ref=x_land.at[a // 2],
            send_sem=bsend.at[a // 2],
            recv_sem=brecv.at[a // 2],
            device_id=(me_x + a - 1, me_y),
            device_id_type=MESH,
        )

    def sides(act, sign):
        for a in range(3):
            for b in (0, 2):

                @pl.when(exists(me_x + a - 1, nx) & exists(me_y + sign * (b - 1), ny))
                def _():
                    act(a, b)

    def column_copy(step, g):
        other = lax.rem(me_y + step, ny)
        return pltpu.make_async_remote_copy(
            src_ref=wpart_ref.at[other, g],
            dst_ref=yland.at[step - 1, g],
            send_sem=ysend.at[step - 1, g],
            recv_sem=yrecv.at[step - 1, g],
            device_id=(me_x, other),
            device_id_type=MESH,
        )

    late = list(range(2, steps))
    kinds = [[0, 1] + late, [1, 0] + late, late + [0, 1], late + [1, 0]]
    orders = [kinds[kind] for kind in KINDS]
    starts = []
    for g in range(groups):
        at = [0]
        for s in range(steps):
            at.append(at[-1] + bits[orders[g][s]] * (nx >> (s + 1)))
        starts.append(at)

    def scatter_copy(g, s):
        half = nx >> (s + 1)
        bit = bits[orders[g][s]]
        away = starts[g][s] + (1 - bit) * half
        return pltpu.make_async_remote_copy(
            src_ref=work.at[g, pl.ds(away, half)],
            dst_ref=xland.at[g, pl.ds(nx - 2 * half, half)],
            send_sem=rsend.at[s, g],
            recv_sem=rrecv.at[s, g],
            device_id=(partners[orders[g][s]], me_y),
            device_id_type=MESH,
        )

    def gather_copy(g, s, landing):
        half = nx >> (s + 1)
        bit = bits[orders[g][s]]
        mine = starts[g][s + 1]
        place = starts[g][s] + (1 - bit) * half if landing else mine
        return pltpu.make_async_remote_copy(
            src_ref=sum_ref.at[g, pl.ds(mine, half)],
            dst_ref=sum_ref.at[g, pl.ds(place, half)],
            send_sem=gsend.at[s, g],
            recv_sem=grecv.at[s, g],
            device_id=(partners[orders[g][s]], me_y),
            device_id_type=MESH,
        )

    for g in range(groups):
        for step in range(1, ny):
            column_copy(step, g).start()
    sides(lambda a, b: side_copy(a, b).start(), 1)

    for g in range(groups):
        value = wpart_ref[me_y, g].astype(jnp.float32)
        for step in range(1, ny):
            column_copy(step, g).wait_recv()
            value = value + yland[step - 1, g].astype(jnp.float32)
        work[g] = value.astype(work.dtype)
        scatter_copy(g, 0).start()

    returned_ref[...] = jnp.zeros(returned_ref.shape, jnp.float32)
    for b in (0, 2):

        @pl.when(exists(me_y + 1 - b, ny))
        def _():
            side_copy(1, b).wait_recv()
            returned_ref[...] += side_land[1, b // 2].astype(jnp.float32)

    for a in (0, 2):

        @pl.when(exists(me_x + a - 1, nx))
        def _():
            for b in (0, 2):
                missing = jnp.logical_not(exists(me_y + 1 - b, ny))

                @pl.when(missing)
                def _():
                    side_land[a, b // 2] = jnp.zeros(side_land.shape[2:], side_land.dtype)

                @pl.when(jnp.logical_not(missing))
                def _():
                    side_copy(a, b).wait_recv()

            column[a // 2] = (
                borrowed_ref[3 * a + 1].astype(jnp.float32)
                + side_land[a, 0].astype(jnp.float32)
                + side_land[a, 1].astype(jnp.float32)
            ).astype(column.dtype)
            back_copy(a).start()

    for s in range(steps):
        half = nx >> (s + 1)
        for g in range(groups):
            scatter_copy(g, s).wait_recv()
            keep = pl.ds(starts[g][s + 1], half)
            value = work[g, keep].astype(jnp.float32) + xland[
                g, pl.ds(nx - 2 * half, half)
            ].astype(jnp.float32)
            if s < steps - 1:
                work[g, keep] = value.astype(work.dtype)
                scatter_copy(g, s + 1).start()
            else:
                sum_ref[g, keep] = value.astype(sum_ref.dtype)
                gather_copy(g, s, False).start()

    for a in (0, 2):

        @pl.when(exists(me_x + 1 - a, nx))
        def _():
            back_copy(a).wait_recv()
            returned_ref[...] += x_land[a // 2].astype(jnp.float32)

    for s in reversed(range(steps)):
        for g in range(groups):
            gather_copy(g, s, True).wait_recv()
            if s > 0:
                gather_copy(g, s - 1, False).start()

    for g in range(groups):
        for step in range(1, ny):
            column_copy(step, g).wait_send()
        for s in range(steps):
            scatter_copy(g, s).wait_send()
            gather_copy(g, s, False).wait_send()
    sides(lambda a, b: side_copy(a, b).wait_send(), 1)
    for a in (0, 2):

        @pl.when(exists(me_x + a - 1, nx))
        def _():
            back_copy(a).wait_send()


def finish_kernel(blocks, send_ref, total_ref, own_ref, returned_ref, weight_ref, feat_ref):
    per, share, width = weight_ref.shape
    rows = own_ref.shape[1]
    for h in range(width // LANES):
        weight_ref[:, :, h * LANES : (h + 1) * LANES] = total_ref[h].reshape(
            per, share, LANES
        ).astype(jnp.float32) * (1.0 / rows)
    at = jnp.minimum(pl.program_id(0), blocks - 1)
    value = own_ref[0]
    for s in range(returned_ref.shape[0]):
        value = value + jnp.where(send_ref[s] == at, returned_ref[s], 0.0)
    feat_ref[0] = value.astype(feat_ref.dtype)


def on_device(
    nx,
    ny,
    features,
    kernel_weight,
    channel_bias,
    send_list,
    rule_source,
    rule_target,
    live_counts,
    out_grad,
):
    feats = features[0, 0]
    blocks, rows, width = feats.shape
    shared = send_list[0, 0]
    shared_count = shared.shape[0]
    kvol, slots = rule_source.shape[2:]
    share = kernel_weight.shape[1]
    bf16, f32 = jnp.bfloat16, jnp.float32
    shape = jax.ShapeDtypeStruct
    vmem = pl.BlockSpec(memory_space=VMEM)
    smem = pl.BlockSpec(memory_space=SMEM)
    dma = pltpu.SemaphoreType.DMA
    squares = 9

    halo, full = pl.pallas_call(
        functools.partial(exchange_kernel, nx, ny),
        out_shape=(
            shape((squares, shared_count, rows, width), bf16),
            shape((kvol, ny, share, width), bf16),
        ),
        in_specs=[smem, vmem, vmem],
        out_specs=(vmem, vmem),
        scratch_shapes=[dma((2,)), dma((2,)), dma((3, 2)), dma((3, 2)), dma((ny,)), dma((ny,))],
        compiler_params=pltpu.CompilerParams(
            collective_id=0, has_side_effects=True, vmem_limit_bytes=VMEM_BYTES
        ),
    )(shared, feats, kernel_weight)

    total_blocks = blocks + (squares - 1) * shared_count
    used = (width // LANES) * kvol * (share // TILE)
    groups = len(KINDS)
    unit = groups * nx
    tiles = -(-used // unit) * unit
    depth = tiles // unit
    outputs, own, borrowed, wpart = pl.pallas_call(
        compute_kernel,
        out_shape=(
            shape((blocks, rows, width), bf16),
            shape((blocks, rows, width), f32),
            shape((squares, shared_count, rows, width), bf16),
            shape((ny, tiles, TILE, LANES), bf16),
        ),
        in_specs=[smem, smem, smem, vmem, vmem, vmem, vmem, vmem],
        out_specs=(vmem, vmem, vmem, vmem),
        scratch_shapes=[
            VMEM((total_blocks, rows, width), bf16),
            VMEM((total_blocks, width, rows), bf16),
            VMEM((blocks + 1, rows, width), f32),
            VMEM((blocks + 1, rows, width), bf16),
            VMEM((total_blocks + 1, rows, width), f32),
        ],
        compiler_params=pltpu.CompilerParams(vmem_limit_bytes=VMEM_BYTES),
    )(
        rule_source[0, 0].T,
        rule_target[0, 0].T,
        live_counts.reshape(-1),
        feats,
        halo,
        full.reshape(kvol, width, width),
        channel_bias.reshape(1, width),
        out_grad[0, 0],
    )

    steps = nx.bit_length() - 1
    block = (depth, TILE, LANES)
    boundary = (shared_count, rows, width)
    total, returned = pl.pallas_call(
        functools.partial(reduce_kernel, nx, ny),
        out_shape=(
            shape((groups, nx) + block, bf16),
            shape(boundary, f32),
        ),
        in_specs=[vmem, vmem],
        out_specs=(vmem, vmem),
        scratch_shapes=[
            VMEM((groups, nx) + block, bf16),
            VMEM((max(ny - 1, 1), groups, nx) + block, bf16),
            VMEM((groups, nx) + block, bf16),
            VMEM((3, 2) + boundary, bf16),
            VMEM((2,) + boundary, bf16),
            VMEM((2,) + boundary, bf16),
            dma((max(ny - 1, 1), groups)),
            dma((max(ny - 1, 1), groups)),
            dma((steps, groups)),
            dma((steps, groups)),
            dma((steps, groups)),
            dma((steps, groups)),
            dma((3, 2)),
            dma((3, 2)),
            dma((2,)),
            dma((2,)),
        ],
        compiler_params=pltpu.CompilerParams(
            collective_id=1, has_side_effects=True, vmem_limit_bytes=VMEM_BYTES
        ),
    )(wpart.reshape((ny, groups, nx) + block), borrowed)

    per = max(p for p in range(1, kvol + 1) if kvol % p == 0 and kvol // p >= blocks)
    halves, share_tiles = width // LANES, share // TILE

    def own_block(i):
        return (jnp.minimum(i, blocks - 1), 0, 0)

    weight_grad, feat_grad = pl.pallas_call(
        functools.partial(finish_kernel, blocks),
        grid=(kvol // per,),
        out_shape=(shape((kvol, share, width), f32), shape((blocks, rows, width), bf16)),
        in_specs=[
            smem,
            pl.BlockSpec((halves, per, share_tiles, TILE, LANES), lambda i: (0, i, 0, 0, 0)),
            pl.BlockSpec((1, rows, width), own_block),
            pl.BlockSpec(boundary, lambda i: (0, 0, 0)),
        ],
        out_specs=(
            pl.BlockSpec((per, share, width), lambda i: (i, 0, 0)),
            pl.BlockSpec((1, rows, width), own_block),
        ),
        compiler_params=pltpu.CompilerParams(vmem_limit_bytes=VMEM_BYTES),
    )(
        shared,
        total.reshape(tiles, TILE, LANES)[:used].reshape(halves, kvol, share_tiles, TILE, LANES),
        own,
        returned,
    )
    return (outputs[None, None], feat_grad[None, None], weight_grad)


def solution(mesh):
    return jax.shard_map(
        functools.partial(on_device, mesh.shape["gx"], mesh.shape["gy"]),
        mesh=mesh,
        in_specs=(
            P("gx", "gy", None, None, None),
            P(None, "gy", None),
            P(),
            P("gx", "gy", None),
            P("gx", "gy", None, None),
            P("gx", "gy", None, None),
            P("gx", "gy", None),
            P("gx", "gy", None, None, None),
        ),
        out_specs=(
            P("gx", "gy", None, None, None),
            P("gx", "gy", None, None, None),
            P(None, "gy", None),
        ),
        check_vma=False,
    )
```

time: 109 us -> 83.7 us (0.77)
  Pallas kernels: 99.7 us -> 79.5 us
  local copies, waits for them, and re-layouts: 6.6 us -> 3.21 us
  other arithmetic: 2.66 us -> 0 us
    pallas_call x1, Pallas kernels: 59.9 us -> 50.6 us  [on_device(): pl.pallas_call(functools.partial(reduce_kernel, nx, ny), out_shape=(shape...]
    pallas_call x1, Pallas kernels: 20.6 us -> 12.2 us  [on_device(): pl.pallas_call(functools.partial(exchange_kernel, nx, ny), out_shape=(sha...]
    pallas_call x1 -> x2, Pallas kernels: 19.2 us -> 16.7 us  [the longest x1 12 us: on_device(): pl.pallas_call(compute_kernel, out_shape=(shape((blocks, rows, width), bf...]
    mul x1 -> x0, local copies, waits for them, and re-layouts: 2.12 us -> none  [on_device(): total.reshape(tiles, TILE, LANES)[:used].reshape(width // LANES, kvol, sh...]
    unnamed x8 -> x18, local copies, waits for them, and re-layouts: 1.56 us -> 3.21 us
    eq x1 -> x0, other arithmetic: 1.3 us -> none  [on_device(): hit = shared[s] == jnp.arange(blocks, dtype=jnp.int32)]
    reshape x2 -> x0, local copies, waits for them, and re-layouts: 1.23 us -> none  [the longest x1 0.61 us: on_device(): rule_source.reshape(-1)]
    broadcast_in_dim x1 -> x0, local copies, waits for them, and re-layouts: 1.12 us -> none  [on_device(): jnp.where(hit[:, None, None], returned[s][None], 0.0)]
where the time goes in v1:
time: 83.7 us; the launch traced here: 83.5 us
  Pallas kernels  79.5 us (95%)
  local copies, waits for them, and re-layouts  3.21 us (4%)
    pallas_call x1, Pallas kernels, on_device(): pl.pallas_call(functools.partial(reduce_kernel, nx, ny), out_shape=(shape...  50.6 us
    pallas_call x1, Pallas kernels, on_device(): pl.pallas_call(functools.partial(exchange_kernel, nx, ny), out_shape=(sha...  12.2 us
    pallas_call x1, Pallas kernels, on_device(): pl.pallas_call(compute_kernel, out_shape=(shape((blocks, rows, width), bf...  12 us
    pallas_call x1, Pallas kernels, on_device(): pl.pallas_call(functools.partial(finish_kernel, blocks), grid=(kvol // pe...  4.7 us
    unnamed x18, local copies, waits for them, and re-layouts  3.21 us

profile of v1, /device:TPU:0, one launch (start us, length us, event | category | flops | bytes accessed | tf_op | source)
XLA Modules:
  0.0 83.5 jit_solution(1927182596280879591)
XLA Ops:
  0.6 0.0 copy-start.8
  0.6 0.0 copy-start.5
  0.7 0.0 copy-start.4
  0.7 0.0 copy-start.7
  0.7 0.0 copy-start
  0.7 1.1 %copy-done = bf16[1,1,8,128,256]{4,3,2,1,0:T(8,128)(2,1)S(1)} copy-done((bf16[1,1,8,128,256]{4,3,2,1,0:T(8,128)(2,1)S(1)}, bf16[1,1,8,128,256]{4,3,2,1,0:T(8,128)(2,1)}, u32[]{:S(2)}) %copy-start) | copy-done | bytes 524312
  1.7 0.0 copy-start.2
  1.7 1.5 %copy-done.2 = bf16[27,128,256]{2,1,0:T(8,128)(2,1)S(1)} copy-done((bf16[27,128,256]{2,1,0:T(8,128)(2,1)S(1)}, bf16[27,128,256]{2,1,0:T(8,128)(2,1)}, u32[]{:S(2)}) %copy-start.2) | copy-done | bytes 1769496
  3.2 0.0 copy-start.6
  3.2 0.7 copy-done.6
  3.9 0.0 copy-start.1
  3.9 0.0 copy-start.3
  3.9 12.2 %shard_map.103 = (bf16[9,2,128,256]{3,2,1,0:T(8,128)(2,1)S(1)}, bf16[27,2,128,256]{3,2,1,0:T(8,128)(2,1)S(1)}) custom-call(s32[2]{0:T(128)S(1)} %bitcast.24, bf16[8,128,256]{2,1,0:T(8,128)(2,1)S(1)} %bitcast.18, bf16[27,128,256]{2,1,0:T(8,128)(2,1)S(1)} %copy-done.2), custom_call_target="tpu_custom_call" | custom-call | tf_op jit(solution)/shard_map/pallas_call | solution.py:498
  16.1 0.0 copy-done.8
  16.1 0.0 copy-done.5
  16.1 0.0 copy-done.4
  16.1 0.0 copy-done.7
  16.1 0.0 copy-done.1
  16.1 0.0 copy-done.3
  16.1 12.0 %shard_map.104 = (bf16[8,128,256]{2,1,0:T(8,128)(2,1)}, f32[8,128,256]{2,1,0:T(8,128)S(1)}, bf16[9,2,128,256]{3,2,1,0:T(8,128)(2,1)S(1)}, bf16[2,432,16,128]{3,2,1,0:T(8,128)(2,1)S(1)}) custom-call(s32[4,27]{1,0:T(4,128)S(1)} %bitcast.22, s32[4,27]{1,0:T(4,128)S(1)} %bitcast.23, s32[27]{0:T(128)S(1)} %bitcast.27, bf16[8,128,256]{2,1,0:T(8,128)(2,1)S(1)} %bitcast.19, ...), custom_call_target="tpu_custom_call" | custom-call | tf_op jit(solution)/shard_map/pallas_call | solution.py:518
  28.2 50.6 %shard_map.105 = (bf16[9,16,3,16,128]{4,3,2,1,0:T(8,128)(2,1)S(1)}, f32[2,128,256]{2,1,0:T(8,128)S(1)}) custom-call(bf16[2,9,16,3,16,128]{5,4,3,2,1,0:T(8,128)(2,1)S(1)} %bitcast.16, bf16[9,2,128,256]{3,2,1,0:T(8,128)(2,1)S(1)} %get-tuple-element.17.borrowed_ref), custom_call_target="tpu_custom_call" | custom-call | tf_op jit(solution)/shard_map/pallas_call | solution.py:550
  78.8 4.7 %shard_map.106 = (f32[27,128,256]{2,1,0:T(8,128)}, bf16[8,128,256]{2,1,0:T(8,128)(2,1)}) custom-call(s32[2]{0:T(128)S(1)} %bitcast.25, bf16[2,27,8,16,128]{4,3,2,1,0:T(8,128)(2,1)S(1)} %bitcast.20, f32[8,128,256]{2,1,0:T(8,128)S(1)} %get-tuple-element.19.own_ref, f32[2,128,256]{2,1,0:T(8,128)S(1)} %get-tuple-element.20.returned_ref), custom_call_target="tpu_custom_call" | custom-call | tf_op jit(solution)/shard_map/pallas_call | solution.py:587
Async XLA Ops:
  0.6 15.5 %copy-start.8 = (s32[1,1,27]{2,1,0:T(1,128)S(1)}, s32[1,1,27]{2,1,0:T(1,128)}, u32[]{:S(2)}) copy-start(s32[1,1,27]{2,1,0:T(1,128)} %param.14) | copy-start | bytes 328
  0.6 15.5 %copy-start.5 = (s32[1,1,27,4]{2,3,1,0:T(4,128)S(1)}, s32[1,1,27,4]{2,3,1,0:T(4,128)}, u32[]{:S(2)}) copy-start(s32[1,1,27,4]{2,3,1,0:T(4,128)} %param.13) | copy-start | bytes 1300
  0.7 15.5 %copy-start.4 = (s32[1,1,27,4]{2,3,1,0:T(4,128)S(1)}, s32[1,1,27,4]{2,3,1,0:T(4,128)}, u32[]{:S(2)}) copy-start(s32[1,1,27,4]{2,3,1,0:T(4,128)} %param.12) | copy-start | bytes 1300
  0.7 15.5 %copy-start.7 = (f32[256]{0:T(256)S(1)}, f32[256]{0:T(256)}, u32[]{:S(2)}) copy-start(f32[256]{0:T(256)} %param.10) | copy-start | bytes 3076
  0.7 1.1 %copy-start = (bf16[1,1,8,128,256]{4,3,2,1,0:T(8,128)(2,1)S(1)}, bf16[1,1,8,128,256]{4,3,2,1,0:T(8,128)(2,1)}, u32[]{:S(2)}) copy-start(bf16[1,1,8,128,256]{4,3,2,1,0:T(8,128)(2,1)} %param.8) | copy-start | bytes 1572868
  1.7 1.5 %copy-start.2 = (bf16[27,128,256]{2,1,0:T(8,128)(2,1)S(1)}, bf16[27,128,256]{2,1,0:T(8,128)(2,1)}, u32[]{:S(2)}) copy-start(bf16[27,128,256]{2,1,0:T(8,128)(2,1)} %weight_ref.1) | copy-start | bytes 5308420
  3.2 0.7 copy-start.6
  3.9 12.3 %copy-start.1 = (bf16[1,1,8,128,256]{4,3,2,1,0:T(8,128)(2,1)S(1)}, bf16[1,1,8,128,256]{4,3,2,1,0:T(8,128)(2,1)}, u32[]{:S(2)}) copy-start(bf16[1,1,8,128,256]{4,3,2,1,0:T(8,128)(2,1)} %param.8) | copy-start | bytes 1572868
  3.9 12.3 %copy-start.3 = (bf16[1,1,8,128,256]{4,3,2,1,0:T(8,128)(2,1)S(1)}, bf16[1,1,8,128,256]{4,3,2,1,0:T(8,128)(2,1)}, u32[]{:S(2)}) copy-start(bf16[1,1,8,128,256]{4,3,2,1,0:T(8,128)(2,1)} %param.15) | copy-start | bytes 1572868

commit v2 on v1

--- a/solution.py
+++ b/solution.py
@@ -13,8 +13,12 @@
 LANES = 128
 TILE = 16
 KINDS = (2, 0, 1, 3, 0, 1, 0, 1, 0)
-UNROLL = 3
+WAVES = (0,) * 9
+STAGGER = 1
+HALO_AT = 4
+UNROLL = 9
 VMEM_BYTES = 28 * 1024 * 1024
+EXCHANGE_BYTES = 28 * 1024 * 1024
 
 
 def greet_neighbours(barrier, me_x, me_y, nx, ny):
@@ -44,15 +48,20 @@
 
 
 def exchange_kernel(
-    nx, ny, send_ref, feats_ref, weight_ref, halo_ref, full_ref, xsend, xrecv, hsend, hrecv, wsend, wrecv
+    nx, ny, send_ref, feats_ref, weight_ref, halo_ref, full_ref, feats, lsem, xsend, xrecv, hsend, hrecv, wsend, wrecv
 ):
     me_x, me_y = lax.axis_index("gx"), lax.axis_index("gy")
     barrier = pltpu.get_barrier_semaphore()
     expected = greet_neighbours(barrier, me_x, me_y, nx, ny) + greet_column(
         barrier, me_x, me_y, ny
     )
+    load = pltpu.make_async_copy(feats_ref, feats, lsem.at[0])
+    load.start()
+    keep = pltpu.make_async_copy(weight_ref, full_ref.at[:, me_y], lsem.at[1])
+    keep.start()
+    load.wait()
     for s in range(halo_ref.shape[1]):
-        halo_ref[4, s] = feats_ref[send_ref[s]]
+        halo_ref[4, s] = feats[send_ref[s]]
     pl.semaphore_wait(barrier, expected)
 
     def x_copy(a, device_x):
@@ -103,7 +112,6 @@
     to_column(1, lambda copy: copy.start())
     for step in range(1, ny):
         weight_copy(step, me_y).start()
-    full_ref[:, me_y] = weight_ref[...]
     blank = jnp.zeros(halo_ref.shape[1:], halo_ref.dtype)
     for a in (0, 2):
         here = exists(me_x + a - 1, nx)
@@ -143,6 +151,7 @@
     for step in range(1, ny):
         weight_copy(step, lax.rem(me_y - step + ny, ny)).wait_recv()
         weight_copy(step, me_y).wait_send()
+    keep.wait()
 
 
 def compute_kernel(
@@ -376,7 +385,7 @@
             column_copy(step, g).start()
     sides(lambda a, b: side_copy(a, b).start(), 1)
 
-    for g in range(groups):
+    def begin(g):
         value = wpart_ref[me_y, g].astype(jnp.float32)
         for step in range(1, ny):
             column_copy(step, g).wait_recv()
@@ -384,6 +393,39 @@
         work[g] = value.astype(work.dtype)
         scatter_copy(g, 0).start()
 
+    def scatter(g, s):
+        half = nx >> (s + 1)
+        scatter_copy(g, s).wait_recv()
+        keep = pl.ds(starts[g][s + 1], half)
+        value = work[g, keep].astype(jnp.float32) + xland[g, pl.ds(nx - 2 * half, half)].astype(
+            jnp.float32
+        )
+        if s < steps - 1:
+            work[g, keep] = value.astype(work.dtype)
+            scatter_copy(g, s + 1).start()
+        else:
+            sum_ref[g, keep] = value.astype(sum_ref.dtype)
+            gather_copy(g, s, False).start()
+
+    def gather(g, s):
+        gather_copy(g, s, True).wait_recv()
+        if s > 0:
+            gather_copy(g, s - 1, False).start()
+
+    events = []
+    for g in range(groups):
+        events.append((WAVES[g] * STAGGER, g, functools.partial(begin, g)))
+        for s in range(steps):
+            events.append((WAVES[g] * STAGGER + s + 1, g, functools.partial(scatter, g, s)))
+            events.append(
+                (WAVES[g] * STAGGER + 2 * steps - s, g, functools.partial(gather, g, s))
+            )
+    events.sort(key=lambda event: event[:2])
+    first = [event[2] for event in events if event[0] < HALO_AT]
+    rest = [event[2] for event in events if event[0] >= HALO_AT]
+    for event in first:
+        event()
+
     returned_ref[...] = jnp.zeros(returned_ref.shape, jnp.float32)
     for b in (0, 2):
 
@@ -414,20 +456,8 @@
             ).astype(column.dtype)
             back_copy(a).start()
 
-    for s in range(steps):
-        half = nx >> (s + 1)
-        for g in range(groups):
-            scatter_copy(g, s).wait_recv()
-            keep = pl.ds(starts[g][s + 1], half)
-            value = work[g, keep].astype(jnp.float32) + xland[
-                g, pl.ds(nx - 2 * half, half)
-            ].astype(jnp.float32)
-            if s < steps - 1:
-                work[g, keep] = value.astype(work.dtype)
-                scatter_copy(g, s + 1).start()
-            else:
-                sum_ref[g, keep] = value.astype(sum_ref.dtype)
-                gather_copy(g, s, False).start()
+    for event in rest:
+        event()
 
     for a in (0, 2):
 
@@ -435,12 +465,6 @@
         def _():
             back_copy(a).wait_recv()
             returned_ref[...] += x_land[a // 2].astype(jnp.float32)
-
-    for s in reversed(range(steps)):
-        for g in range(groups):
-            gather_copy(g, s, True).wait_recv()
-            if s > 0:
-                gather_copy(g, s - 1, False).start()
 
     for g in range(groups):
         for step in range(1, ny):
@@ -456,18 +480,33 @@
             back_copy(a).wait_send()
 
 
-def finish_kernel(blocks, send_ref, total_ref, own_ref, returned_ref, weight_ref, feat_ref):
-    per, share, width = weight_ref.shape
-    rows = own_ref.shape[1]
-    for h in range(width // LANES):
-        weight_ref[:, :, h * LANES : (h + 1) * LANES] = total_ref[h].reshape(
-            per, share, LANES
-        ).astype(jnp.float32) * (1.0 / rows)
-    at = jnp.minimum(pl.program_id(0), blocks - 1)
-    value = own_ref[0]
-    for s in range(returned_ref.shape[0]):
-        value = value + jnp.where(send_ref[s] == at, returned_ref[s], 0.0)
-    feat_ref[0] = value.astype(feat_ref.dtype)
+def finish_kernel(
+    send_ref, total_ref, own_ref, returned_ref, weight_ref, feat_ref, wide, feats, wsem, fsem
+):
+    chunks = wsem.shape[0]
+    kvol, share, width = wide.shape
+    per = kvol // chunks
+    blocks, rows = own_ref.shape[:2]
+    copies = []
+    for c in range(chunks):
+        at = pl.ds(c * per, per)
+        for h in range(width // LANES):
+            wide[at, :, h * LANES : (h + 1) * LANES] = total_ref[h, at].reshape(
+                per, share, LANES
+            ).astype(jnp.float32) * (1.0 / rows)
+        copy = pltpu.make_async_copy(wide.at[at], weight_ref.at[at], wsem.at[c])
+        copy.start()
+        copies.append(copy)
+    for b in range(blocks):
+        value = own_ref[b]
+        for s in range(returned_ref.shape[0]):
+            value = value + jnp.where(send_ref[s] == b, returned_ref[s], 0.0)
+        feats[b] = value.astype(feats.dtype)
+        copy = pltpu.make_async_copy(feats.at[b], feat_ref.at[b], fsem.at[b])
+        copy.start()
+        copies.append(copy)
+    for copy in copies:
+        copy.wait()
 
 
 def on_device(
@@ -492,6 +531,7 @@
     shape = jax.ShapeDtypeStruct
     vmem = pl.BlockSpec(memory_space=VMEM)
     smem = pl.BlockSpec(memory_space=SMEM)
+    hbm = pl.BlockSpec(memory_space=pltpu.HBM)
     dma = pltpu.SemaphoreType.DMA
     squares = 9
 
@@ -501,11 +541,20 @@
             shape((squares, shared_count, rows, width), bf16),
             shape((kvol, ny, share, width), bf16),
         ),
-        in_specs=[smem, vmem, vmem],
+        in_specs=[smem, hbm, hbm],
         out_specs=(vmem, vmem),
-        scratch_shapes=[dma((2,)), dma((2,)), dma((3, 2)), dma((3, 2)), dma((ny,)), dma((ny,))],
+        scratch_shapes=[
+            VMEM((blocks, rows, width), bf16),
+            dma((2,)),
+            dma((2,)),
+            dma((2,)),
+            dma((3, 2)),
+            dma((3, 2)),
+            dma((ny,)),
+            dma((ny,)),
+        ],
         compiler_params=pltpu.CompilerParams(
-            collective_id=0, has_side_effects=True, vmem_limit_bytes=VMEM_BYTES
+            collective_id=0, has_side_effects=True, vmem_limit_bytes=EXCHANGE_BYTES
         ),
     )(shared, feats, kernel_weight)
 
@@ -578,26 +627,19 @@
         ),
     )(wpart.reshape((ny, groups, nx) + block), borrowed)
 
-    per = max(p for p in range(1, kvol + 1) if kvol % p == 0 and kvol // p >= blocks)
     halves, share_tiles = width // LANES, share // TILE
-
-    def own_block(i):
-        return (jnp.minimum(i, blocks - 1), 0, 0)
-
+    chunks = max(c for c in range(1, 10) if kvol % c == 0)
     weight_grad, feat_grad = pl.pallas_call(
-        functools.partial(finish_kernel, blocks),
-        grid=(kvol // per,),
+        finish_kernel,
         out_shape=(shape((kvol, share, width), f32), shape((blocks, rows, width), bf16)),
-        in_specs=[
-            smem,
-            pl.BlockSpec((halves, per, share_tiles, TILE, LANES), lambda i: (0, i, 0, 0, 0)),
-            pl.BlockSpec((1, rows, width), own_block),
-            pl.BlockSpec(boundary, lambda i: (0, 0, 0)),
+        in_specs=[smem, vmem, vmem, vmem],
+        out_specs=(hbm, hbm),
+        scratch_shapes=[
+            VMEM((kvol, share, width), f32),
+            VMEM((blocks, rows, width), bf16),
+            dma((chunks,)),
+            dma((blocks,)),
         ],
-        out_specs=(
-            pl.BlockSpec((per, share, width), lambda i: (i, 0, 0)),
-            pl.BlockSpec((1, rows, width), own_block),
-        ),
         compiler_params=pltpu.CompilerParams(vmem_limit_bytes=VMEM_BYTES),
     )(
         shared,

time: 83.7 us -> 74.4 us (0.89)
  Pallas kernels: 79.5 us -> 70.3 us
    pallas_call x1, Pallas kernels: 50.6 us -> 45.8 us  [on_device(): pl.pallas_call(functools.partial(reduce_kernel, nx, ny), out_shape=(shape...]
    pallas_call x1, Pallas kernels: 12 us -> 9.64 us  [on_device(): pl.pallas_call(compute_kernel, out_shape=(shape((blocks, rows, width), bf...]
    pallas_call x1, Pallas kernels: 4.7 us -> 2.66 us  [on_device(): pl.pallas_call(finish_kernel, out_shape=(shape((kvol, share, width), f32)...]
where the time goes in v2:
time: 74.4 us; the launch traced here: 74.3 us
  Pallas kernels  70.3 us (94%)
  local copies, waits for them, and re-layouts  3.21 us (4%)
    pallas_call x1, Pallas kernels, on_device(): pl.pallas_call(functools.partial(reduce_kernel, nx, ny), out_shape=(shape...  45.8 us
    pallas_call x1, Pallas kernels, on_device(): pl.pallas_call(functools.partial(exchange_kernel, nx, ny), out_shape=(sha...  12.2 us
    pallas_call x1, Pallas kernels, on_device(): pl.pallas_call(compute_kernel, out_shape=(shape((blocks, rows, width), bf...  9.64 us
    unnamed x18, local copies, waits for them, and re-layouts  3.21 us
    pallas_call x1, Pallas kernels, on_device(): pl.pallas_call(finish_kernel, out_shape=(shape((kvol, share, width), f32)...  2.66 us

profile of v2, /device:TPU:0, one launch (start us, length us, event | category | flops | bytes accessed | tf_op | source)
XLA Modules:
  0.0 74.3 jit_solution(14464254750256536962)
XLA Ops:
  0.6 0.0 copy-start.8
  0.6 0.0 copy-start.5
  0.7 0.0 copy-start.4
  0.7 0.0 copy-start.7
  0.7 0.0 copy-start
  0.7 1.1 %copy-done = bf16[1,1,8,128,256]{4,3,2,1,0:T(8,128)(2,1)S(1)} copy-done((bf16[1,1,8,128,256]{4,3,2,1,0:T(8,128)(2,1)S(1)}, bf16[1,1,8,128,256]{4,3,2,1,0:T(8,128)(2,1)}, u32[]{:S(2)}) %copy-start) | copy-done | bytes 524312
  1.7 0.0 copy-start.2
  1.7 1.5 %copy-done.2 = bf16[27,128,256]{2,1,0:T(8,128)(2,1)S(1)} copy-done((bf16[27,128,256]{2,1,0:T(8,128)(2,1)S(1)}, bf16[27,128,256]{2,1,0:T(8,128)(2,1)}, u32[]{:S(2)}) %copy-start.2) | copy-done | bytes 1769496
  3.2 0.0 copy-start.6
  3.2 0.7 copy-done.6
  3.9 0.0 copy-start.1
  3.9 0.0 copy-start.3
  3.9 12.2 %shard_map.103 = (bf16[9,2,128,256]{3,2,1,0:T(8,128)(2,1)S(1)}, bf16[27,2,128,256]{3,2,1,0:T(8,128)(2,1)S(1)}) custom-call(s32[2]{0:T(128)S(1)} %bitcast.24, bf16[8,128,256]{2,1,0:T(8,128)(2,1)S(1)} %bitcast.18, bf16[27,128,256]{2,1,0:T(8,128)(2,1)S(1)} %copy-done.2), custom_call_target="tpu_custom_call" | custom-call | tf_op jit(solution)/shard_map/pallas_call | solution.py:538
  16.1 0.0 copy-done.8
  16.1 0.0 copy-done.5
  16.1 0.0 copy-done.4
  16.1 0.0 copy-done.7
  16.1 0.0 copy-done.1
  16.2 0.0 copy-done.3
  16.2 9.6 %shard_map.104 = (bf16[8,128,256]{2,1,0:T(8,128)(2,1)}, f32[8,128,256]{2,1,0:T(8,128)S(1)}, bf16[9,2,128,256]{3,2,1,0:T(8,128)(2,1)S(1)}, bf16[2,432,16,128]{3,2,1,0:T(8,128)(2,1)S(1)}) custom-call(s32[4,27]{1,0:T(4,128)S(1)} %bitcast.22, s32[4,27]{1,0:T(4,128)S(1)} %bitcast.23, s32[27]{0:T(128)S(1)} %bitcast.27, bf16[8,128,256]{2,1,0:T(8,128)(2,1)S(1)} %bitcast.19, ...), custom_call_target="tpu_custom_call" | custom-call | tf_op jit(solution)/shard_map/pallas_call | solution.py:567
  25.8 45.8 %shard_map.105 = (bf16[9,16,3,16,128]{4,3,2,1,0:T(8,128)(2,1)S(1)}, f32[2,128,256]{2,1,0:T(8,128)S(1)}) custom-call(bf16[2,9,16,3,16,128]{5,4,3,2,1,0:T(8,128)(2,1)S(1)} %bitcast.16, bf16[9,2,128,256]{3,2,1,0:T(8,128)(2,1)S(1)} %get-tuple-element.17.borrowed_ref), custom_call_target="tpu_custom_call" | custom-call | tf_op jit(solution)/shard_map/pallas_call | solution.py:599
  71.6 2.7 %shard_map.106 = (f32[27,128,256]{2,1,0:T(8,128)}, bf16[8,128,256]{2,1,0:T(8,128)(2,1)}) custom-call(s32[2]{0:T(128)S(1)} %bitcast.25, bf16[2,27,8,16,128]{4,3,2,1,0:T(8,128)(2,1)S(1)} %bitcast.20, f32[8,128,256]{2,1,0:T(8,128)S(1)} %get-tuple-element.19.own_ref, f32[2,128,256]{2,1,0:T(8,128)S(1)} %get-tuple-element.20.returned_ref), custom_call_target="tpu_custom_call" | custom-call | tf_op jit(solution)/shard_map/pallas_call | solution.py:632
Async XLA Ops:
  0.6 15.5 %copy-start.8 = (s32[1,1,27]{2,1,0:T(1,128)S(1)}, s32[1,1,27]{2,1,0:T(1,128)}, u32[]{:S(2)}) copy-start(s32[1,1,27]{2,1,0:T(1,128)} %param.14) | copy-start | bytes 328
  0.6 15.5 %copy-start.5 = (s32[1,1,27,4]{2,3,1,0:T(4,128)S(1)}, s32[1,1,27,4]{2,3,1,0:T(4,128)}, u32[]{:S(2)}) copy-start(s32[1,1,27,4]{2,3,1,0:T(4,128)} %param.13) | copy-start | bytes 1300
  0.7 15.5 %copy-start.4 = (s32[1,1,27,4]{2,3,1,0:T(4,128)S(1)}, s32[1,1,27,4]{2,3,1,0:T(4,128)}, u32[]{:S(2)}) copy-start(s32[1,1,27,4]{2,3,1,0:T(4,128)} %param.12) | copy-start | bytes 1300
  0.7 15.5 %copy-start.7 = (f32[256]{0:T(256)S(1)}, f32[256]{0:T(256)}, u32[]{:S(2)}) copy-start(f32[256]{0:T(256)} %param.10) | copy-start | bytes 3076
  0.7 1.1 %copy-start = (bf16[1,1,8,128,256]{4,3,2,1,0:T(8,128)(2,1)S(1)}, bf16[1,1,8,128,256]{4,3,2,1,0:T(8,128)(2,1)}, u32[]{:S(2)}) copy-start(bf16[1,1,8,128,256]{4,3,2,1,0:T(8,128)(2,1)} %param.8) | copy-start | bytes 1572868
  1.7 1.5 %copy-start.2 = (bf16[27,128,256]{2,1,0:T(8,128)(2,1)S(1)}, bf16[27,128,256]{2,1,0:T(8,128)(2,1)}, u32[]{:S(2)}) copy-start(bf16[27,128,256]{2,1,0:T(8,128)(2,1)} %weight_ref.1) | copy-start | bytes 5308420
  3.2 0.7 copy-start.6
  3.9 12.3 %copy-start.1 = (bf16[1,1,8,128,256]{4,3,2,1,0:T(8,128)(2,1)S(1)}, bf16[1,1,8,128,256]{4,3,2,1,0:T(8,128)(2,1)}, u32[]{:S(2)}) copy-start(bf16[1,1,8,128,256]{4,3,2,1,0:T(8,128)(2,1)} %param.8) | copy-start | bytes 1572868
  3.9 12.3 %copy-start.3 = (bf16[1,1,8,128,256]{4,3,2,1,0:T(8,128)(2,1)S(1)}, bf16[1,1,8,128,256]{4,3,2,1,0:T(8,128)(2,1)}, u32[]{:S(2)}) copy-start(bf16[1,1,8,128,256]{4,3,2,1,0:T(8,128)(2,1)} %param.15) | copy-start | bytes 1572868
